TPU v7x, 32 devices: a whole 2x2x4 slice. The times are simulated.
32 devices in a mesh: seq: 4 (over y, x), head: 8 (over z, core).
Axes of the slice: x: 2, y: 2, z: 4, core: 2. Of those that a mesh axis runs over, the one named last changes fastest.
Arguments:
- inputs: bfloat16 [4096, 6144], P('seq', 'head'), may hold values from -6 to 6
- projection: bfloat16 [6144, 3, 4096], P('seq', None, 'head'), may hold values from -0.078125 to 0.078125
- cotangent: bfloat16 [4096, 4096], P('seq', 'head'), may hold values from -0.3125 to 0.3125
- log_decay: float32 [32, 4096], P('head', 'seq'), may hold values from -0.7 to 0
- document_starts: int32 [4], replicated, may hold values from 0 to 3328, as said below
Outputs:
- input_gradient: bfloat16 [4096, 6144], P('seq', 'head')
- weight_gradient: bfloat16 [6144, 3, 4096], P('seq', None, 'head')
Inputs may be any that keep to these rules, and one draw needn't show every extreme that they name: `document_starts`: strictly increasing; the first is 0 and the last is (3) * 1024 + 256.
All inputs are finite; a program needn't handle non-finite values.
Results may differ from a plain program's by a relative error of at most 0.02.
Values may be sent and summed in bfloat16 or wider, within the bound.
A program may use at most 192 MiB of HBM per device.

v0:
```python
import jax
import jax.numpy as jnp
from jax import lax
from jax.sharding import PartitionSpec as P

HEAD_DIM = 128
BLOCK = 256


def hop(array, axis, flip):
    return lax.ppermute(array, axis, [(i, i ^ flip) for i in range(lax.axis_size(axis))])


def gather_states(packed, axis):
    length = lax.axis_size(axis)
    if length != 4:
        return lax.all_gather(packed, axis)
    place = lax.axis_index(axis)
    parts = [packed] + [hop(packed, axis, flip) for flip in range(1, length)]
    rows = []
    for at in range(length):
        row = parts[0]
        for flip in range(1, length):
            row = jnp.where(place == at ^ flip, parts[flip], row)
        rows.append(row)
    return rows


def combine_devices(states, decays, place, reverse):
    length = len(decays)
    total = jnp.zeros_like(states[0])
    for k in range(length):
        at = length - 1 - k if reverse else k
        reached = at > place if reverse else at < place
        total = jnp.where(reached, decays[at][:, None, None] * total + states[at], total)
    return total


def gather_rows(part, axis):
    length, place, rows = (lax.axis_size(axis), lax.axis_index(axis), part.shape[1])
    if length != 4:
        whole = lax.all_gather(part, axis, axis=1, tiled=True)
        return [(0, 0, whole)]
    half = rows // 2
    low, high = (part[:, :half], part[:, half:])
    x_high = hop(high, axis, 1)
    y_low = hop(low, axis, 2)
    x_low = hop(low, axis, 1)
    y_high = hop(high, axis, 2)
    d_low = hop(y_low, axis, 1)
    d_high = hop(x_high, axis, 2)
    return [
        (place, 0, low),
        (place, half, high),
        (place ^ 1, half, x_high),
        (place ^ 2, 0, y_low),
        (place ^ 1, 0, x_low),
        (place ^ 2, half, y_high),
        (place ^ 3, 0, d_low),
        (place ^ 3, half, d_high),
    ]


def scatter_rows(partial, axis, rows):
    length, place = (lax.axis_size(axis), lax.axis_index(axis))
    if length != 4:
        return lax.psum_scatter(partial(0, 0, rows * length), axis, scatter_dimension=1, tiled=True)
    half = rows // 2

    def add(*terms):
        return sum((term.astype(jnp.float32) for term in terms)).astype(jnp.bfloat16)

    far_low = hop(partial(place ^ 3, 0, half), axis, 1)
    far_high = hop(partial(place ^ 3, half, half), axis, 2)
    x_low = hop(partial(place ^ 1, 0, half), axis, 1)
    y_high = hop(partial(place ^ 2, half, half), axis, 2)
    x_high = hop(add(partial(place ^ 1, half, half), far_high), axis, 1)
    y_low = hop(add(partial(place ^ 2, 0, half), far_low), axis, 2)
    own_low, own_high = (partial(place, 0, half), partial(place, half, half))
    return jnp.concatenate([add(own_low, x_low, y_low), add(own_high, x_high, y_high)], axis=1)


def silu_slope(point):
    sigma = jax.nn.sigmoid(point)
    return sigma * (1.0 + point * (1.0 - sigma))


def block_factors(decay_sum, doc_index, doc_begin):
    inside = jnp.arange(doc_index.shape[-1], dtype=jnp.int32)
    causal = inside[:, None] >= inside[None, :]
    same_doc = (doc_index[:, :, None] == doc_index[:, None, :]) & causal[None]
    spread = jnp.minimum(decay_sum[..., :, None] - decay_sum[..., None, :], 0.0)
    pair_weight = jnp.where(same_doc[None], jnp.exp(spread), 0.0)
    to_end = jnp.where(
        (doc_index == doc_index[:, -1:])[None], jnp.exp(decay_sum[..., -1:] - decay_sum), 0.0
    )
    began_flag = doc_index == doc_index[:, :1] - doc_begin[:, :1]
    from_start = jnp.where(began_flag[None], jnp.exp(decay_sum), 0.0)
    return (pair_weight, to_end, from_start, from_start[..., -1])


def block_pair(decay):
    high = decay.astype(jnp.bfloat16)
    low = (decay - high.astype(jnp.float32)).astype(jnp.bfloat16)
    pair = jnp.stack([high, low], axis=1)
    slab = jnp.pad(pair, ((0, HEAD_DIM - pair.shape[0]), (0, HEAD_DIM - 2)))
    return slab[None]


def combine_states(earlier, later):
    return (earlier[0] * later[0], later[0][:, None, None] * earlier[1] + later[1])


def body(inputs, projection, cotangent, log_decay, document_starts):
    tokens = inputs.shape[0]
    heads_here = log_decay.shape[0]
    local_cols = cotangent.shape[1]
    blocks = tokens // BLOCK
    query_scale = HEAD_DIM ** (-0.5)
    features = lax.all_gather(inputs, "head", axis=1, tiled=True)
    rows = projection.shape[0]
    blocks_w = gather_rows(projection.transpose(1, 0, 2), "seq")

    def feature_rows(owner, first, count):
        return lax.dynamic_slice_in_dim(features, owner * rows + first, count, axis=1)

    projected = sum(
        (
            jnp.einsum(
                "td,kdc->ktc",
                feature_rows(owner, first, block.shape[1]),
                block,
                preferred_element_type=jnp.float32,
            )
            for owner, first, block in blocks_w
        )
    )
    queries = (jax.nn.silu(projected[0]) * query_scale).astype(jnp.bfloat16)
    keys = jax.nn.silu(projected[1]).astype(jnp.bfloat16)
    values = projected[2].astype(jnp.bfloat16)

    def split_blocks(table):
        return table.reshape(blocks, BLOCK, heads_here, HEAD_DIM).transpose(2, 0, 1, 3)

    def merge_blocks(table):
        return table.transpose(1, 2, 0, 3).reshape(tokens, local_cols)

    queries_b = split_blocks(queries)
    keys_b = split_blocks(keys)
    values_b = split_blocks(values)
    upstream = split_blocks(cotangent)
    offset = lax.axis_index("seq") * tokens
    positions = offset + jnp.arange(tokens, dtype=jnp.int32)
    doc_index = (
        jnp.sum((document_starts[None, :] <= positions[:, None]).astype(jnp.int32), axis=1) - 1
    )
    doc_begin = jnp.any(document_starts[None, :] == positions[:, None], axis=1).astype(jnp.int32)
    decay_sum = jnp.cumsum(log_decay.reshape(heads_here, blocks, BLOCK), axis=-1)
    pair_weight, to_end, from_start, block_decay = block_factors(
        decay_sum, doc_index.reshape(blocks, BLOCK), doc_begin.reshape(blocks, BLOCK)
    )
    keys_weighted = (keys_b.astype(jnp.float32) * to_end[..., None]).astype(jnp.bfloat16)
    queries_weighted = (queries_b.astype(jnp.float32) * from_start[..., None]).astype(jnp.bfloat16)
    key_state = jnp.einsum(
        "hbse,hbsf->hbef", keys_weighted, values_b, preferred_element_type=jnp.float32
    )
    query_state = jnp.einsum(
        "hbte,hbtf->hbef", queries_weighted, upstream, preferred_element_type=jnp.float32
    )

    def local_step(carry, item):
        return (combine_states(carry, item), carry)

    ones = jnp.ones((heads_here,), jnp.float32)
    empty = jnp.zeros((heads_here, HEAD_DIM, HEAD_DIM), jnp.float32)
    (device_decay, device_keys), (prior_decay, prior_keys) = lax.scan(
        local_step, (ones, empty), (block_decay.T, key_state.swapaxes(0, 1))
    )
    (device_decay_back, device_query), (later_decay, later_query) = lax.scan(
        local_step, (ones, empty), (block_decay.T, query_state.swapaxes(0, 1)), reverse=True
    )
    place = lax.axis_index("seq")
    rough = block_pair(device_decay)
    packed = jnp.concatenate(
        [device_keys.astype(jnp.bfloat16), device_query.astype(jnp.bfloat16), rough]
    )
    everything = gather_states(packed, "seq")
    everything = [everything[k].astype(jnp.float32) for k in range(lax.axis_size("seq"))]
    decays = [
        part[2 * heads_here, :heads_here, 0] + part[2 * heads_here, :heads_here, 1]
        for part in everything
    ]
    forward_in = combine_devices([part[:heads_here] for part in everything], decays, place, False)
    backward_in = combine_devices(
        [part[heads_here : 2 * heads_here] for part in everything], decays, place, True
    )
    state_before = (
        (prior_decay[:, :, None, None] * forward_in[None] + prior_keys)
        .swapaxes(0, 1)
        .astype(jnp.bfloat16)
    )
    state_after = (
        (later_decay[:, :, None, None] * backward_in[None] + later_query)
        .swapaxes(0, 1)
        .astype(jnp.bfloat16)
    )
    query_key = (
        jnp.einsum("hbte,hbse->hbts", queries_b, keys_b, preferred_element_type=jnp.float32)
        * pair_weight
    ).astype(jnp.bfloat16)
    value_score = (
        jnp.einsum("hbtf,hbsf->hbts", upstream, values_b, preferred_element_type=jnp.float32)
        * pair_weight
    ).astype(jnp.bfloat16)
    query_gradient = jnp.einsum(
        "hbts,hbse->hbte", value_score, keys_b, preferred_element_type=jnp.float32
    ) + from_start[..., None] * jnp.einsum(
        "hbtf,hbef->hbte", upstream, state_before, preferred_element_type=jnp.float32
    )
    key_gradient = jnp.einsum(
        "hbts,hbte->hbse", value_score, queries_b, preferred_element_type=jnp.float32
    ) + to_end[..., None] * jnp.einsum(
        "hbsf,hbef->hbse", values_b, state_after, preferred_element_type=jnp.float32
    )
    value_gradient = jnp.einsum(
        "hbts,hbtf->hbsf", query_key, upstream, preferred_element_type=jnp.float32
    ) + to_end[..., None] * jnp.einsum(
        "hbse,hbef->hbsf", keys_b, state_after, preferred_element_type=jnp.float32
    )
    project_gradient = jnp.stack(
        [
            merge_blocks(query_gradient) * silu_slope(projected[0]) * query_scale,
            merge_blocks(key_gradient) * silu_slope(projected[1]),
            merge_blocks(value_gradient),
        ],
        axis=0,
    ).astype(jnp.bfloat16)

    def weight_partial(owner, first, count):
        return jnp.einsum(
            "td,ktc->kdc",
            feature_rows(owner, first, count),
            project_gradient,
            preferred_element_type=jnp.float32,
        ).astype(jnp.bfloat16)

    partial_value = jnp.zeros((tokens, features.shape[1]), jnp.bfloat16)
    for owner, first, block in blocks_w:
        piece = jnp.einsum(
            "ktc,kdc->td", project_gradient, block, preferred_element_type=jnp.float32
        ).astype(jnp.bfloat16)
        partial_value = lax.dynamic_update_slice_in_dim(
            partial_value, piece, owner * rows + first, axis=1
        )
    input_gradient = lax.psum_scatter(partial_value, "head", scatter_dimension=1, tiled=True)
    weight_gradient = scatter_rows(weight_partial, "seq", rows).transpose(1, 0, 2)
    return (input_gradient, weight_gradient)


def solution(mesh):
    placed = (P("seq", "head"), P("seq", None, "head"), P("seq", "head"), P("head", "seq"), P())
    return jax.shard_map(
        body,
        mesh=mesh,
        in_specs=placed,
        out_specs=(P("seq", "head"), P("seq", None, "head")),
        check_vma=False,
    )
```

profile of v0, /device:TPU:0, one launch (start us, length us, event | category | flops | bytes accessed | tf_op | source)
XLA Modules:
  0.0 527.8 jit_solution(1366227272367069007)
XLA Ops:
  8.0 5.3 %fusion.148 = (bf16[3,768,512]{2,1,0:T(8,128)(2,1)}, bf16[3,768,512]{2,1,0:T(8,128)(2,1)}) fusion(bf16[3,1536,512]{2,1,0:T(8,128)(2,1)} %bitcast.245), kind=kLoop, calls=%fused_computation.224 | loop fusion | bytes 9437184 | tf_op jit(solution)/shard_map/slice | solution.py:45
  18.5 4.8 reduce-window.6
  27.3 41.3 %collective-permute-done.1 = bf16[3,768,512]{2,1,0:T(8,128)(2,1)} collective-permute-done((bf16[3,768,512]{2,1,0:T(8,128)(2,1)}, bf16[3,768,512]{2,1,0:T(8,128)(2,1)}, u32[]{:S(2)}, u32[]{:S(2)}) %collective-permute-start.1) | collective-permute-done | bytes 2359328 | tf_op jit(solution)/shard_map/ppermute | solution.py:11
  73.2 55.9 %all-gather.2.cloned.1.call-done = bf16[1024,6144]{1,0:T(8,128)(2,1)} async-done(((bf16[1024,768]{1,0:T(8,128)(2,1)}), bf16[1024,6144]{1,0:T(8,128)(2,1)}) %all-gather.2.cloned.1.call-update) | async-done | bytes 12582928 | tf_op jit(solution)/shard_map/all_gather | solution.py:120
  129.1 7.5 %fusion.43 = f32[1024,3,512]{2,0,1:T(8,128)} fusion(bf16[3,768,512]{2,1,0:T(8,128)(2,1)} %collective-permute-done, bf16[1024,6144]{1,0:T(8,128)(2,1)} %all-gather.2.cloned.1.call-done, s32[]{:T(128)S(6)} %select_n.169), kind=kOutput, calls=%fused_computation.81 | convolution fusion | flops 2415919104 | bytes 10223620 | tf_op jit(solution)/shard_map/td,kdc->ktc/dot_general | solution.py:129
  136.6 7.5 %fusion.40 = f32[1024,3,512]{2,0,1:T(8,128)} fusion(bf16[3,768,512]{2,1,0:T(8,128)(2,1)} %collective-permute-done.1, bf16[1024,6144]{1,0:T(8,128)(2,1)} %all-gather.2.cloned.1.call-done, s32[]{:T(128)S(6)} %select_n.170), kind=kOutput, calls=%fused_computation.78 | convolution fusion | flops 2415919104 | bytes 10223620 | tf_op jit(solution)/shard_map/td,kdc->ktc/dot_general | solution.py:129
  144.2 4.6 fusion.47
  148.8 4.6 fusion.51
  153.4 17.0 %collective-permute-done.4 = bf16[3,768,512]{2,1,0:T(8,128)(2,1)} collective-permute-done((bf16[3,768,512]{2,1,0:T(8,128)(2,1)}, bf16[3,768,512]{2,1,0:T(8,128)(2,1)}, u32[]{:S(2)}, u32[]{:S(2)}) %collective-permute-start.4) | collective-permute-done | bytes 2359328 | tf_op jit(solution)/shard_map/ppermute | solution.py:11
  170.4 6.1 %fusion.31 = f32[1024,3,512]{2,0,1:T(8,128)} fusion(bf16[3,768,512]{2,1,0:T(8,128)(2,1)} %collective-permute-done.4, bf16[1024,6144]{1,0:T(8,128)(2,1)S(1)} %bitcast.256, s32[]{:T(128)S(6)} %select_n.173), kind=kOutput, calls=%fused_computation.69 | convolution fusion | flops 2415919104 | bytes 10223620 | tf_op jit(solution)/shard_map/td,kdc->ktc/dot_general | solution.py:129
  176.6 6.2 %fusion.34 = f32[1024,3,512]{2,0,1:T(8,128)} fusion(bf16[3,768,512]{2,1,0:T(8,128)(2,1)} %collective-permute-done.3, bf16[1024,6144]{1,0:T(8,128)(2,1)S(1)} %bitcast.256, s32[]{:T(128)S(6)} %select_n.172), kind=kOutput, calls=%fused_computation.72 | convolution fusion | flops 2415919104 | bytes 10223620 | tf_op jit(solution)/shard_map/td,kdc->ktc/dot_general | solution.py:129
  182.7 6.2 %fusion.37 = f32[1024,3,512]{2,0,1:T(8,128)} fusion(bf16[3,768,512]{2,1,0:T(8,128)(2,1)} %collective-permute-done.2, bf16[1024,6144]{1,0:T(8,128)(2,1)S(1)} %bitcast.256, s32[]{:T(128)S(6)} %select_n.171), kind=kOutput, calls=%fused_computation.75 | convolution fusion | flops 2415919104 | bytes 10223620 | tf_op jit(solution)/shard_map/td,kdc->ktc/dot_general | solution.py:129
  190.3 18.9 %add_bitcast_fusion = f32[3,1024,512]{2,1,0:T(8,128)} fusion(f32[1024,3,512]{2,0,1:T(8,128)} %fusion.31, f32[1024,3,512]{2,0,1:T(8,128)} %fusion.34, f32[1024,3,512]{2,0,1:T(8,128)} %fusion.37, f32[1024,3,512]{2,0,1:T(8,128)} %fusion.40, f32[1024,3,512]{2,0,1:T(8,128)} %fusion.43, f32[1024,3,512]{2,0,1:T(8,128)} %fusion.51, f32[1024,3,512]{2,0,1:T(8,128)} %fusion.47, ...), kind=kOutput, calls=%fused_computation.14 | convolution fusion | flops 2426929152 | bytes 54263812 | tf_op jit(solution)/shard_map/td,kdc->ktc/dot_general | solution.py:129
  227.6 7.3 %while.38 = (s32[]{:T(128)}, f32[4]{0:T(128)S(1)}, f32[4,128,128]{2,1,0:T(8,128)S(1)}, f32[4,4]{1,0:T(4,128)S(1)}, f32[4,4,128,128]{3,2,1,0:T(8,128)}, /*index=5...) while((s32[]{:T(128)}, f32[4]{0:T(128)S(1)}, ...), condition=%wide.region_5.6_spmd.clone, body=%wide.region_4.5_spmd.clone.sunk | while | flops 262155 | bytes 1311477 | solution.py:176
  235.1 4.3 convolution_bitcast_fusion
  240.4 7.4 %while.39 = (s32[]{:T(128)}, f32[4]{0:T(128)S(1)}, f32[4,128,128]{2,1,0:T(8,128)S(1)}, f32[4,4]{1,0:T(4,128)S(1)}, f32[4,4,128,128]{3,2,1,0:T(8,128)}, /*index=5...) while((s32[]{:T(128)}, f32[4]{0:T(128)S(1)}, ...), condition=%wide.region_7.8_spmd.clone, body=%wide.region_6.7_spmd.clone.sunk | while | flops 262156 | bytes 1310989 | solution.py:179
  255.9 5.5 %fusion.53 = f32[4,4,256,128]{3,2,1,0:T(8,128)} fusion(f32[4,4,256]{2,1,0:T(4,128)S(1)} %reduce_window_sum.30, pred[4,256,256]{1,2,0:T(8,128)(4,1)S(1)} %copy-done.19, bf16[4,256,4,128]{3,1,0,2:T(8,128)(2,1)S(1)} %multiply_convert_fusion.6, bf16[4,256,4,128]{3,2,1,0:T(4,128)(2,1)} %reshape.196, f32[4,256,4,128]{3,2,1,0:T(4,128)} %squeeze.48), kind=kOutput, calls=%fused_computation.91 | convolution fusion | flops 545259520 | bytes 6569984 | tf_op jit(solution)/shard_map/hbts,hbtf->hbsf/dot_general | solution.py:225
  292.1 5.4 %multiply_convert_fusion.2 = (bf16[1,1024,512]{2,1,0:T(8,128)(2,1)S(1)}, bf16[1,1024,512]{2,1,0:T(8,128)(2,1)}) fusion(f32[1,1024,512]{2,1,0:T(8,128)} %reshape.199, f32[3,1024,512]{2,1,0:T(8,128)} %add_bitcast_fusion, f32[1,1024,512]{2,1,0:T(8,128)S(1)} %copy-done.2), kind=kLoop, calls=%fused_computation.52 | loop fusion | flops 9961472 | bytes 10485760 | tf_op jit(solution)/shard_map/convert.6
  297.5 6.1 %broadcast_in_dim.91 = bf16[1024,6144]{1,0:T(8,128)(2,1)} broadcast(bf16[]{:T(256)} %constant.85.clone.1), dimensions={} | broadcast | bytes 12582914 | tf_op jit(solution)/shard_map/broadcast_in_dim | solution.py:247
  303.6 5.5 %fusion.17 = bf16[1024,6144]{1,0:T(8,128)(2,1)} fusion(bf16[1024,6144]{1,0:T(8,128)(2,1)} %broadcast_in_dim.91, s32[]{:T(128)S(6)} %select_n.167, bf16[3,1536,512]{2,1,0:T(8,128)(2,1)S(1)} %bitcast.252, bf16[1,1024,512]{2,1,0:T(8,128)(2,1)} %stack_reshape.4, bf16[1,1024,512]{2,1,0:T(8,128)(2,1)} %get-tuple-element.341, ...), kind=kOutput, calls=%fused_computation.57 | convolution fusion | flops 2419851264 | bytes 7077892 | tf_op jit(solution)/shard_map/ktc,kdc->td/dot_general | solution.py:249
  313.1 5.5 %fusion.19 = bf16[1024,6144]{1,0:T(8,128)(2,1)} fusion(bf16[1024,6144]{1,0:T(8,128)(2,1)} %fusion.18, s32[]{:T(128)S(6)} %select_n.169, bf16[3,768,512]{2,1,0:T(8,128)(2,1)} %collective-permute-done, bf16[1,1024,512]{2,1,0:T(8,128)(2,1)S(1)} %copy-done.15, bf16[1,1024,512]{2,1,0:T(8,128)(2,1)S(1)} %copy-done.12, ...), kind=kOutput, calls=%fused_computation.59 | convolution fusion | flops 2419851264 | bytes 7077892 | tf_op jit(solution)/shard_map/ktc,kdc->td/dot_general | solution.py:249
  318.5 5.5 %fusion.20 = bf16[1024,6144]{1,0:T(8,128)(2,1)} fusion(bf16[1024,6144]{1,0:T(8,128)(2,1)} %fusion.19, s32[]{:T(128)S(6)} %select_n.170, bf16[3,768,512]{2,1,0:T(8,128)(2,1)} %collective-permute-done.1, bf16[1,1024,512]{2,1,0:T(8,128)(2,1)S(1)} %copy-done.15, bf16[1,1024,512]{2,1,0:T(8,128)(2,1)S(1)} %copy-done.12, ...), kind=kOutput, calls=%fused_computation.60 | convolution fusion | flops 2419851264 | bytes 7077892 | tf_op jit(solution)/shard_map/ktc,kdc->td/dot_general | solution.py:249
  324.0 5.9 %fusion.21 = bf16[1024,6144]{1,0:T(8,128)(2,1)} fusion(bf16[1024,6144]{1,0:T(8,128)(2,1)} %fusion.20, s32[]{:T(128)S(6)} %select_n.171, bf16[3,768,512]{2,1,0:T(8,128)(2,1)} %collective-permute-done.2, bf16[1,1024,512]{2,1,0:T(8,128)(2,1)S(1)} %copy-done.15, bf16[1,1024,512]{2,1,0:T(8,128)(2,1)S(1)} %copy-done.12, ...), kind=kOutput, calls=%fused_computation.61 | convolution fusion | flops 2419851264 | bytes 7077892 | tf_op jit(solution)/shard_map/ktc,kdc->td/dot_general | solution.py:249
  330.0 5.5 %fusion.22 = bf16[1024,6144]{1,0:T(8,128)(2,1)} fusion(bf16[1024,6144]{1,0:T(8,128)(2,1)} %fusion.21, s32[]{:T(128)S(6)} %select_n.172, bf16[3,768,512]{2,1,0:T(8,128)(2,1)} %collective-permute-done.3, bf16[1,1024,512]{2,1,0:T(8,128)(2,1)S(1)} %copy-done.15, bf16[1,1024,512]{2,1,0:T(8,128)(2,1)S(1)} %copy-done.12, ...), kind=kOutput, calls=%fused_computation.62 | convolution fusion | flops 2419851264 | bytes 7077892 | tf_op jit(solution)/shard_map/ktc,kdc->td/dot_general | solution.py:249
  335.5 5.6 %fusion.23 = bf16[1024,6144]{1,0:T(8,128)(2,1)} fusion(bf16[1024,6144]{1,0:T(8,128)(2,1)} %fusion.22, s32[]{:T(128)S(6)} %select_n.173, bf16[3,768,512]{2,1,0:T(8,128)(2,1)} %collective-permute-done.4, bf16[1,1024,512]{2,1,0:T(8,128)(2,1)S(1)} %copy-done.15, bf16[1,1024,512]{2,1,0:T(8,128)(2,1)S(1)} %copy-done.12, ...), kind=kOutput, calls=%fused_computation.63 | convolution fusion | flops 2419851264 | bytes 7077892 | tf_op jit(solution)/shard_map/ktc,kdc->td/dot_general | solution.py:249
  346.8 4.6 convert_bitcast_fusion.2
  352.9 4.6 convert_bitcast_fusion.1
  368.1 37.5 %collective-permute-done.10 = bf16[3,768,512]{1,2,0:T(8,128)(2,1)S(1)} collective-permute-done((bf16[3,768,512]{1,2,0:T(8,128)(2,1)S(1)}, bf16[3,768,512]{1,2,0:T(8,128)(2,1)S(1)}, u32[]{:S(2)}, u32[]{:S(2)}) %collective-permute-start.10) | collective-permute-done | bytes 2359328 | tf_op jit(solution)/shard_map/ppermute | solution.py:11
  411.7 4.3 fusion.6
  423.6 32.6 %collective-permute-done.9 = bf16[3,768,512]{1,2,0:T(8,128)(2,1)S(1)} collective-permute-done((bf16[3,768,512]{1,2,0:T(8,128)(2,1)S(1)}, bf16[3,768,512]{1,2,0:T(8,128)(2,1)S(1)}, u32[]{:S(2)}, u32[]{:S(2)}) %collective-permute-start.9) | collective-permute-done | bytes 2359328 | tf_op jit(solution)/shard_map/ppermute | solution.py:11
  456.2 53.3 %collective-permute-done.11 = bf16[3,768,512]{1,2,0:T(8,128)(2,1)S(1)} collective-permute-done((bf16[3,768,512]{1,2,0:T(8,128)(2,1)S(1)}, bf16[3,768,512]{1,2,0:T(8,128)(2,1)S(1)}, u32[]{:S(2)}, u32[]{:S(2)}) %collective-permute-start.11) | collective-permute-done | bytes 2359328 | tf_op jit(solution)/shard_map/ppermute | solution.py:11
  514.1 6.6 %copy.172 = bf16[1536,3,512]{2,0,1:T(8,128)(2,1)} copy(bf16[1536,3,512]{0,2,1:T(8,128)(2,1)} %maximum_bitcast_fusion) | data formatting | bytes 9437184
  (210 shorter events, 128.8 us)
Async XLA Ops:
  7.2 121.9 %all-gather.2.cloned.1.call-start = ((), (), s32[]{:S(2)}) async-start(), calls=%async_computation.1 | async-start | bytes 14155776 | tf_op jit(solution)/shard_map/all_gather | solution.py:120
  7.9 512.8 %reduce-scatter.2.cloned.1.call-start = ((), (), s32[]{:S(2)}) async-start(), calls=%async_computation.2 | async-start | bytes 14155776 | tf_op jit(solution)/shard_map/reduce_scatter | solution.py:255
  7.9 10.4 %copy-start.21 = (s32[4]{0:T(128)S(1)}, s32[4]{0:T(128)}, u32[]{:S(2)}) copy-start(s32[4]{0:T(128)} %param.13) | copy-start | bytes 52
  8.0 10.5 %copy-start.20 = (f32[4,1024]{1,0:T(4,128)S(1)}, f32[4,1024]{1,0:T(4,128)}, u32[]{:S(2)}) copy-start(f32[4,1024]{1,0:T(4,128)} %param.12) | copy-start | bytes 49156
  8.0 15.8 %copy-start.14 = (bf16[1024,512]{1,0:T(8,128)(2,1)S(1)}, bf16[1024,512]{1,0:T(8,128)(2,1)}, u32[]{:S(2)}) copy-start(bf16[1024,512]{1,0:T(8,128)(2,1)} %param.11) | copy-start | bytes 3145732
  13.3 55.4 %collective-permute-start.1 = (bf16[3,768,512]{2,1,0:T(8,128)(2,1)}, bf16[3,768,512]{2,1,0:T(8,128)(2,1)}, u32[]{:S(2)}, u32[]{:S(2)}) collective-permute-start(bf16[3,768,512]{2,1,0:T(8,128)(2,1)} %get-tuple-element.345), channel_id=1, source_target_pairs={{0,16},{8,24},{16,0},{24,8},{1,17},{9,25},{17,1},{25,9},{2,18},{10... | collective-permute-start | bytes 7077896 | tf_op jit(solution)/shard_map/ppermute | solution.py:11
  16.3 55.4 %collective-permute-start = (bf16[3,768,512]{2,1,0:T(8,128)(2,1)}, bf16[3,768,512]{2,1,0:T(8,128)(2,1)}, u32[]{:S(2)}, u32[]{:S(2)}) collective-permute-start(bf16[3,768,512]{2,1,0:T(8,128)(2,1)} %get-tuple-element.344), channel_id=1, source_target_pairs={{0,8},{8,0},{16,24},{24,16},{1,9},{9,1},{17,25},{25,17},{2,10},{10... | collective-permute-start | bytes 7077896 | tf_op jit(solution)/shard_map/ppermute | solution.py:11
  17.8 158.8 %collective-permute-start.3 = (bf16[3,768,512]{2,1,0:T(8,128)(2,1)}, bf16[3,768,512]{2,1,0:T(8,128)(2,1)}, u32[]{:S(2)}, u32[]{:S(2)}) collective-permute-start(bf16[3,768,512]{2,1,0:T(8,128)(2,1)} %get-tuple-element.344), channel_id=1, source_target_pairs={{0,16},{8,24},{16,0},{24,8},{1,17},{9,25},{17,1},{25,9},{2,18},{10... | collective-permute-start | bytes 7077896 | tf_op jit(solution)/shard_map/ppermute | solution.py:11
  18.3 164.4 %collective-permute-start.2 = (bf16[3,768,512]{2,1,0:T(8,128)(2,1)}, bf16[3,768,512]{2,1,0:T(8,128)(2,1)}, u32[]{:S(2)}, u32[]{:S(2)}) collective-permute-start(bf16[3,768,512]{2,1,0:T(8,128)(2,1)} %get-tuple-element.345), channel_id=1, source_target_pairs={{0,8},{8,0},{16,24},{24,16},{1,9},{9,1},{17,25},{25,17},{2,10},{10... | collective-permute-start | bytes 7077896 | tf_op jit(solution)/shard_map/ppermute | solution.py:11
  68.7 101.8 %collective-permute-start.4 = (bf16[3,768,512]{2,1,0:T(8,128)(2,1)}, bf16[3,768,512]{2,1,0:T(8,128)(2,1)}, u32[]{:S(2)}, u32[]{:S(2)}) collective-permute-start(bf16[3,768,512]{2,1,0:T(8,128)(2,1)} %collective-permute-done.1), channel_id=1, source_target_pairs={{0,8},{8,0},{16,24},{24,16},{1,9},{9,1},{17,25},{25,17},{2,10},{10... | collective-permute-start | bytes 7077896 | tf_op jit(solution)/shard_map/ppermute | solution.py:11
  71.6 117.2 %collective-permute-start.5 = (bf16[3,768,512]{2,1,0:T(8,128)(2,1)}, bf16[3,768,512]{2,1,0:T(8,128)(2,1)S(1)}, u32[]{:S(2)}, u32[]{:S(2)}) collective-permute-start(bf16[3,768,512]{2,1,0:T(8,128)(2,1)} %collective-permute-done), channel_id=1, source_target_pairs={{0,16},{8,24},{16,0},{24,8},{1,17},{9,25},{17,1},{25,9},{2,18},{10... | collective-permute-start | bytes 7077896 | tf_op jit(solution)/shard_map/ppermute | solution.py:11
  129.1 15.1 %slice-start = ((s8[4718592]{0:T(1024)(128)(4,1)}), s8[4194304]{0:T(1024)(128)(4,1)S(1)}, s32[]{:S(2)}) async-start(s8[4718592]{0:T(1024)(128)(4,1)} %bitcast.246), calls=%async_computation.3 | async-start | bytes 8388608
  129.1 15.1 %slice-start.4 = ((s8[12582912]{0:T(1024)(128)(4,1)}), s8[4194304]{0:T(1024)(128)(4,1)S(1)}, s32[]{:S(2)}) async-start(s8[12582912]{0:T(1024)(128)(4,1)} %bitcast.255), calls=%async_computation.7 | async-start | bytes 8388608
  129.1 15.1 %slice-start.5 = ((s8[12582912]{0:T(1024)(128)(4,1)}), s8[4194304]{0:T(1024)(128)(4,1)S(1)}, s32[]{:S(2)}) async-start(s8[12582912]{0:T(1024)(128)(4,1)} %bitcast.255), calls=%async_computation.8 | async-start | bytes 8388608
  136.6 7.5 %slice-start.1 = ((s8[4718592]{0:T(1024)(128)(4,1)}), s8[524288]{0:T(1024)(128)(4,1)S(1)}, s32[]{:S(2)}) async-start(s8[4718592]{0:T(1024)(128)(4,1)} %bitcast.246), calls=%async_computation.4 | async-start | bytes 1048576
  136.6 7.5 %slice-start.6 = ((s8[12582912]{0:T(1024)(128)(4,1)}), s8[4194304]{0:T(1024)(128)(4,1)S(1)}, s32[]{:S(2)}) async-start(s8[12582912]{0:T(1024)(128)(4,1)} %bitcast.255), calls=%async_computation.9 | async-start | bytes 8388608
  248.6 7.3 %copy-start.19 = (pred[4,256,256]{1,2,0:T(8,128)(4,1)S(1)}, pred[4,256,256]{1,2,0:T(8,128)(4,1)}, u32[]{:S(2)}) copy-start(pred[4,256,256]{1,2,0:T(8,128)(4,1)} %compare_and_fusion) | copy-start | bytes 786436
  248.6 18.2 %collective-permute-start.6 = (bf16[9,128,128]{2,1,0:T(8,128)(2,1)}, bf16[9,128,128]{2,1,0:T(8,128)(2,1)S(1)}, u32[]{:S(2)}, u32[]{:S(2)}) collective-permute-start(bf16[9,128,128]{2,1,0:T(8,128)(2,1)} %pad_maximum_fusion.1), channel_id=1, source_target_pairs={{0,24},{8,16},{16,8},{24,0},{1,25},{9,17},{17,9},{25,1},{2,26},{10... | collective-permute-start | bytes 884744 | tf_op jit(solution)/shard_map/ppermute | solution.py:11
  250.0 16.8 %collective-permute-start.7 = (bf16[9,128,128]{2,1,0:T(8,128)(2,1)}, bf16[9,128,128]{2,1,0:T(8,128)(2,1)S(1)}, u32[]{:S(2)}, u32[]{:S(2)}) collective-permute-start(bf16[9,128,128]{2,1,0:T(8,128)(2,1)} %pad_maximum_fusion.1), channel_id=1, source_target_pairs={{0,16},{8,24},{16,0},{24,8},{1,17},{9,25},{17,1},{25,9},{2,18},{10... | collective-permute-start | bytes 884744 | tf_op jit(solution)/shard_map/ppermute | solution.py:11
  251.6 16.7 %collective-permute-start.8 = (bf16[9,128,128]{2,1,0:T(8,128)(2,1)}, bf16[9,128,128]{2,1,0:T(8,128)(2,1)}, u32[]{:S(2)}, u32[]{:S(2)}) collective-permute-start(bf16[9,128,128]{2,1,0:T(8,128)(2,1)} %pad_maximum_fusion.1), channel_id=1, source_target_pairs={{0,8},{8,0},{16,24},{24,16},{1,9},{9,1},{17,25},{25,17},{2,10},{10... | collective-permute-start | bytes 884744 | tf_op jit(solution)/shard_map/ppermute | solution.py:11
  292.1 11.5 %slice-start.2 = ((s8[4718592]{0:T(1024)(128)(4,1)}), s8[524288]{0:T(1024)(128)(4,1)S(1)}, s32[]{:S(2)}) async-start(s8[4718592]{0:T(1024)(128)(4,1)} %bitcast.250), calls=%async_computation.5 | async-start | bytes 1048576
  297.5 43.6 %copy-start.10 = (bf16[1,1024,512]{2,1,0:T(8,128)(2,1)}, bf16[1,1024,512]{2,1,0:T(8,128)(2,1)S(1)}, u32[]{:S(2)}) copy-start(bf16[1,1024,512]{2,1,0:T(8,128)(2,1)S(1)} %get-tuple-element.340) | copy-start | bytes 3145732
  297.5 6.1 %slice-start.3 = ((s8[4718592]{0:T(1024)(128)(4,1)}), s8[4194304]{0:T(1024)(128)(4,1)S(1)}, s32[]{:S(2)}) async-start(s8[4718592]{0:T(1024)(128)(4,1)} %bitcast.250), calls=%async_computation.6 | async-start | bytes 8388608
  346.8 11.7 %slice-start.7 = ((s8[12582912]{0:T(1024)(128)(4,1)}), s8[4194304]{0:T(1024)(128)(4,1)S(1)}, s32[]{:S(2)}) async-start(s8[12582912]{0:T(1024)(128)(4,1)} %bitcast.257), calls=%async_computation.10 | async-start | bytes 8388608
  346.8 11.7 %slice-start.8 = ((s8[12582912]{0:T(1024)(128)(4,1)}), s8[4194304]{0:T(1024)(128)(4,1)S(1)}, s32[]{:S(2)}) async-start(s8[12582912]{0:T(1024)(128)(4,1)} %bitcast.257), calls=%async_computation.11 | async-start | bytes 8388608
  351.3 7.2 %slice-start.9 = ((s8[12582912]{0:T(1024)(128)(4,1)}), s8[4194304]{0:T(1024)(128)(4,1)S(1)}, s32[]{:S(2)}) async-start(s8[12582912]{0:T(1024)(128)(4,1)} %bitcast.257), calls=%async_computation.12 | async-start | bytes 8388608
  351.4 54.2 %collective-permute-start.10 = (bf16[3,768,512]{1,2,0:T(8,128)(2,1)S(1)}, bf16[3,768,512]{1,2,0:T(8,128)(2,1)S(1)}, u32[]{:S(2)}, u32[]{:S(2)}) collective-permute-start(bf16[3,768,512]{1,2,0:T(8,128)(2,1)S(1)} %convert_bitcast_fusion.2), channel_id=1, source_target_pairs={{0,8},{8,0},{16,24},{24,16},{1,9},{9,1},{17,25},{25,17},{2,10},{10... | collective-permute-start | bytes 7077896 | tf_op jit(solution)/shard_map/ppermute | solution.py:11
  357.5 54.2 %collective-permute-start.12 = (bf16[3,768,512]{1,2,0:T(8,128)(2,1)S(1)}, bf16[3,768,512]{1,2,0:T(8,128)(2,1)S(1)}, u32[]{:S(2)}, u32[]{:S(2)}) collective-permute-start(bf16[3,768,512]{1,2,0:T(8,128)(2,1)S(1)} %convert_bitcast_fusion.1), channel_id=1, source_target_pairs={{0,16},{8,24},{16,0},{24,8},{1,17},{9,25},{17,1},{25,9},{2,18},{10... | collective-permute-start | bytes 7077896 | tf_op jit(solution)/shard_map/ppermute | solution.py:11
  361.6 94.6 %collective-permute-start.9 = (bf16[3,768,512]{1,2,0:T(8,128)(2,1)S(1)}, bf16[3,768,512]{1,2,0:T(8,128)(2,1)S(1)}, u32[]{:S(2)}, u32[]{:S(2)}) collective-permute-start(bf16[3,768,512]{1,2,0:T(8,128)(2,1)S(1)} %convert_bitcast_fusion.3), channel_id=1, source_target_pairs={{0,8},{8,0},{16,24},{24,16},{1,9},{9,1},{17,25},{25,17},{2,10},{10... | collective-permute-start | bytes 7077896 | tf_op jit(solution)/shard_map/ppermute | solution.py:11
  366.4 144.1 %collective-permute-start.14 = (bf16[3,768,512]{1,2,0:T(8,128)(2,1)}, bf16[3,768,512]{1,2,0:T(8,128)(2,1)S(1)}, u32[]{:S(2)}, u32[]{:S(2)}) collective-permute-start(bf16[3,768,512]{1,2,0:T(8,128)(2,1)} %convert_bitcast_fusion), channel_id=1, source_target_pairs={{0,16},{8,24},{16,0},{24,8},{1,17},{9,25},{17,1},{25,9},{2,18},{10... | collective-permute-start | bytes 7077896 | tf_op jit(solution)/shard_map/ppermute | solution.py:11
  408.7 100.7 %collective-permute-start.11 = (bf16[3,768,512]{1,2,0:T(8,128)(2,1)S(1)}, bf16[3,768,512]{1,2,0:T(8,128)(2,1)S(1)}, u32[]{:S(2)}, u32[]{:S(2)}) collective-permute-start(bf16[3,768,512]{1,2,0:T(8,128)(2,1)S(1)} %fusion.9), channel_id=1, source_target_pairs={{0,16},{8,24},{16,0},{24,8},{1,17},{9,25},{17,1},{25,9},{2,18},{10... | collective-permute-start | bytes 7077896 | tf_op jit(solution)/shard_map/ppermute | solution.py:11
  416.0 94.5 %collective-permute-start.13 = (bf16[3,768,512]{1,2,0:T(8,128)(2,1)}, bf16[3,768,512]{1,2,0:T(8,128)(2,1)S(1)}, u32[]{:S(2)}, u32[]{:S(2)}) collective-permute-start(bf16[3,768,512]{1,2,0:T(8,128)(2,1)} %fusion.6), channel_id=1, source_target_pairs={{0,8},{8,0},{16,24},{24,16},{1,9},{9,1},{17,25},{25,17},{2,10},{10... | collective-permute-start | bytes 7077896 | tf_op jit(solution)/shard_map/ppermute | solution.py:11
  (17 other events, 44.5 us)
Sparse Core Ops, SparseCore 0:
  9.6 119.4 all-gather.1
  345.1 129.5 reduce-scatter.1
where the time goes:
time: 538 us; the launch traced here: 528 us
  waiting for transfers between devices  241 us (45%)
  matrix products  160 us (30%)
  local copies, waits for them, and re-layouts  55.6 us (10%)
  other arithmetic  37.3 us (7%)
  starting transfers between devices  18.8 us (3%)
  between operations  14.7 us (3%)
    ppermute x15, waiting for transfers between devices, hop(): lax.ppermute(array, axis, [(i, i ^ flip) for i in range(lax.axis_size(axi...  184 us
    dot_general x8, matrix products, body(): jnp.einsum('td,kdc->ktc', feature_rows(owner, first, block.shape[1]), blo...  61.6 us
    all_gather x1, waiting for transfers between devices, body(): features = lax.all_gather(inputs, 'head', axis=1, tiled=True)  55.9 us
    dot_general x8, matrix products, body(): jnp.einsum('ktc,kdc->td', project_gradient, block, preferred_element_type...  41.3 us
    dot_general x8, matrix products, weight_partial(): jnp.einsum('td,ktc->kdc', feature_rows(owner, first, count), project_grad...  29.8 us
    ppermute x15, starting transfers between devices, hop(): lax.ppermute(array, axis, [(i, i ^ flip) for i in range(lax.axis_size(axi...  18.7 us
    unnamed x66, local copies, waits for them, and re-layouts  12 us
  transfers between devices with their start and end apart: 17, of which 7 were waited for; matrix products, arithmetic and copies ran while one was open for 22% of the time, Pallas kernels for 0%

commit v1 on v0

--- a/solution.py
+++ b/solution.py
@@ -5,6 +5,28 @@
 
 HEAD_DIM = 128
 BLOCK = 256
+
+
+def joined_along(tiles, dim):
+    tiles = jnp.moveaxis(tiles, 0, dim)
+    shape = tiles.shape
+    return tiles.reshape(*shape[:dim], shape[dim] * shape[dim + 1], *shape[dim + 2 :])
+
+
+def doubled(array, axis):
+    size = lax.axis_size(axis)
+    parts = array[None]
+    for level in range(size.bit_length() - 1):
+        bit = 1 << level
+        other = lax.ppermute(parts, axis, [(i, i ^ bit) for i in range(size)])
+        both = jnp.stack([parts, other])
+        upper = lax.axis_index(axis) >> level & 1
+        parts = jnp.where(upper == 0, both, both[::-1]).reshape(-1, *array.shape)
+    return parts
+
+
+def doubled_up(array, axis, dim):
+    return joined_along(doubled(array, axis), dim)
 
 
 def hop(array, axis, flip):
@@ -117,7 +139,7 @@
     local_cols = cotangent.shape[1]
     blocks = tokens // BLOCK
     query_scale = HEAD_DIM ** (-0.5)
-    features = lax.all_gather(inputs, "head", axis=1, tiled=True)
+    features = doubled_up(inputs, "head", 1)
     rows = projection.shape[0]
     blocks_w = gather_rows(projection.transpose(1, 0, 2), "seq")
 

time: 538 us -> 759 us (1.41)
  waiting for transfers between devices: 241 us -> 448 us
  other arithmetic: 37.3 us -> 57.6 us
    ppermute x0 -> x3, waiting for transfers between devices: none -> 233 us  [doubled(): other = lax.ppermute(parts, axis, [(i, i ^ bit) for i in range(size)])]
    all_gather x1 -> x0, waiting for transfers between devices: 55.9 us -> none  [body(): features = lax.all_gather(inputs, 'head', axis=1, tiled=True)]
    ppermute x15, waiting for transfers between devices: 184 us -> 214 us  [hop(): lax.ppermute(array, axis, [(i, i ^ flip) for i in range(lax.axis_size(axi...]
    another operation x4 -> x8, other arithmetic: 10.3 us -> 23.4 us  [the longest x4 12.9 us: doubled(): both = jnp.stack([parts, other])]
  transfers between devices with their start and end apart: 17 -> 19, of which waited for: 7 -> 8; matrix products, arithmetic and copies ran while one was open for 22% -> 16% of each run, Pallas kernels for 0% -> 0%
where the time goes in v1:
time: 759 us; the launch traced here: 754 us
  waiting for transfers between devices  448 us (59%)
  matrix products  155 us (20%)
  other arithmetic  57.6 us (8%)
  local copies, waits for them, and re-layouts  55.1 us (7%)
  starting transfers between devices  23.9 us (3%)
  between operations  14.8 us (2%)
    ppermute x3, waiting for transfers between devices, doubled(): other = lax.ppermute(parts, axis, [(i, i ^ bit) for i in range(size)])  233 us
    ppermute x15, waiting for transfers between devices, hop(): lax.ppermute(array, axis, [(i, i ^ flip) for i in range(lax.axis_size(axi...  214 us
    dot_general x8, matrix products, body(): jnp.einsum('td,kdc->ktc', feature_rows(owner, first, block.shape[1]), blo...  57.9 us
    dot_general x8, matrix products, body(): jnp.einsum('ktc,kdc->td', project_gradient, block, preferred_element_type...  39.4 us
    dot_general x8, matrix products, weight_partial(): jnp.einsum('td,ktc->kdc', feature_rows(owner, first, count), project_grad...  30.4 us
    ppermute x15, starting transfers between devices, hop(): lax.ppermute(array, axis, [(i, i ^ flip) for i in range(lax.axis_size(axi...  17.6 us
  transfers between devices with their start and end apart: 19, of which 8 were waited for; matrix products, arithmetic and copies ran while one was open for 16% of the time, Pallas kernels for 0%

profile of v1, /device:TPU:0, one launch (start us, length us, event | category | flops | bytes accessed | tf_op | source)
XLA Modules:
  0.0 754.3 jit_solution(4688926568974932525)
XLA Ops:
  18.0 68.7 %collective-permute-done.1 = bf16[2,1024,768]{2,1,0:T(8,128)(2,1)} collective-permute-done((bf16[2,1024,768]{2,1,0:T(8,128)(2,1)}, bf16[2,1024,768]{2,1,0:T(8,128)(2,1)}, u32[]{:S(2)}, u32[]{:S(2)}) %collective-permute-start.1) | collective-permute-done | bytes 3145760 | tf_op jit(solution)/shard_map/ppermute | solution.py:21
  103.2 5.0 reduce-window.6
  113.2 90.1 %collective-permute-done.4 = bf16[3,768,512]{2,1,0:T(8,128)(2,1)} collective-permute-done((bf16[3,768,512]{2,1,0:T(8,128)(2,1)}, bf16[3,768,512]{2,1,0:T(8,128)(2,1)}, u32[]{:S(2)}, u32[]{:S(2)}) %collective-permute-start.4) | collective-permute-done | bytes 2359328 | tf_op jit(solution)/shard_map/ppermute | solution.py:33
  205.3 161.1 %collective-permute-done.2 = bf16[4,1024,768]{2,1,0:T(8,128)(2,1)} collective-permute-done((bf16[4,1024,768]{2,1,0:T(8,128)(2,1)}, bf16[4,1024,768]{2,1,0:T(8,128)(2,1)}, u32[]{:S(2)}, u32[]{:S(2)}) %collective-permute-start.2) | collective-permute-done | bytes 6291488 | tf_op jit(solution)/shard_map/ppermute | solution.py:21
  366.5 6.2 pad_maximum_fusion
  377.9 5.3 fusion.49
  383.1 4.6 fusion.53
  387.7 6.1 fusion.45
  393.9 6.2 fusion.42
  400.1 6.1 fusion.36
  406.2 4.5 fusion.33
  410.7 6.2 fusion.39
  418.2 19.0 %add_bitcast_fusion = f32[3,1024,512]{2,1,0:T(8,128)} fusion(f32[1024,3,512]{2,0,1:T(8,128)} %fusion.33, f32[1024,3,512]{2,0,1:T(8,128)} %fusion.36, f32[1024,3,512]{2,0,1:T(8,128)} %fusion.39, f32[1024,3,512]{2,0,1:T(8,128)} %fusion.42, f32[1024,3,512]{2,0,1:T(8,128)} %fusion.45, f32[1024,3,512]{2,0,1:T(8,128)} %fusion.53, f32[1024,3,512]{2,0,1:T(8,128)} %fusion.49, ...), kind=kOutput, calls=%fused_computation.18 | convolution fusion | flops 2426929152 | bytes 54263812 | tf_op jit(solution)/shard_map/td,kdc->ktc/dot_general | solution.py:151
  455.6 7.3 while.38
  463.1 4.2 convolution_bitcast_fusion
  468.5 7.4 while.39
  484.1 5.4 fusion.55
  520.3 5.4 multiply_convert_fusion.2
  525.7 6.1 broadcast_in_dim.94
  531.8 5.6 fusion.19
  541.3 5.5 fusion.21
  546.8 5.5 fusion.22
  552.3 5.6 fusion.23
  557.9 5.6 fusion.24
  573.2 4.6 convert_bitcast_fusion.2
  579.1 5.1 convert_bitcast_fusion.1
  594.1 37.8 %collective-permute-done.13 = bf16[3,768,512]{1,2,0:T(8,128)(2,1)S(1)} collective-permute-done((bf16[3,768,512]{1,2,0:T(8,128)(2,1)S(1)}, bf16[3,768,512]{1,2,0:T(8,128)(2,1)S(1)}, u32[]{:S(2)}, u32[]{:S(2)}) %collective-permute-start.13) | collective-permute-done | bytes 2359328 | tf_op jit(solution)/shard_map/ppermute | solution.py:33
  632.0 4.1 fusion.9
  638.5 4.3 fusion.6
  650.5 32.1 %collective-permute-done.12 = bf16[3,768,512]{1,2,0:T(8,128)(2,1)S(1)} collective-permute-done((bf16[3,768,512]{1,2,0:T(8,128)(2,1)S(1)}, bf16[3,768,512]{1,2,0:T(8,128)(2,1)S(1)}, u32[]{:S(2)}, u32[]{:S(2)}) %collective-permute-start.12) | collective-permute-done | bytes 2359328 | tf_op jit(solution)/shard_map/ppermute | solution.py:33
  682.5 53.6 %collective-permute-done.14 = bf16[3,768,512]{1,2,0:T(8,128)(2,1)S(1)} collective-permute-done((bf16[3,768,512]{1,2,0:T(8,128)(2,1)}, bf16[3,768,512]{1,2,0:T(8,128)(2,1)S(1)}, u32[]{:S(2)}, u32[]{:S(2)}) %collective-permute-start.14) | collective-permute-done | bytes 2359328 | tf_op jit(solution)/shard_map/ppermute | solution.py:33
  740.6 6.6 copy.176
  (224 shorter events, 153.2 us)
Async XLA Ops:
  7.2 740.0 %reduce-scatter.2.cloned.1.call-start = ((), (), s32[]{:S(2)}) async-start(), calls=%async_computation.1 | async-start | bytes 14155776 | tf_op jit(solution)/shard_map/reduce_scatter | solution.py:277
  7.2 3.8 collective-permute-start
  15.1 71.7 %collective-permute-start.1 = (bf16[2,1024,768]{2,1,0:T(8,128)(2,1)}, bf16[2,1024,768]{2,1,0:T(8,128)(2,1)}, u32[]{:S(2)}, u32[]{:S(2)}) collective-permute-start(bf16[2,1024,768]{2,1,0:T(8,128)(2,1)} %get-tuple-element.347), channel_id=1, source_target_pairs={{0,2},{1,3},{2,0},{3,1},{4,6},{5,7},{6,4},{7,5},{8,10},{9,11},{10,... | collective-permute-start | bytes 9437192 | tf_op jit(solution)/shard_map/ppermute | solution.py:21
  86.7 9.4 %slice-start.3 = ((s8[4718592]{0:T(1024)(128)(4,1)}), s8[4194304]{0:T(1024)(128)(4,1)S(1)}, s32[]{:S(2)}) async-start(s8[4718592]{0:T(1024)(128)(4,1)} %bitcast.281), calls=%async_computation.5 | async-start | bytes 8388608
  89.3 6.8 slice-start.4
  93.4 273.1 %collective-permute-start.2 = (bf16[4,1024,768]{2,1,0:T(8,128)(2,1)}, bf16[4,1024,768]{2,1,0:T(8,128)(2,1)}, u32[]{:S(2)}, u32[]{:S(2)}) collective-permute-start(bf16[4,1024,768]{2,1,0:T(8,128)(2,1)} %bitcast.7), channel_id=1, source_target_pairs={{0,4},{1,5},{2,6},{3,7},{4,0},{5,1},{6,2},{7,3},{8,12},{9,13},{10,... | collective-permute-start | bytes 18874376 | tf_op jit(solution)/shard_map/ppermute | solution.py:21
  96.1 6.9 copy-start.22
  96.1 7.1 copy-start.21
  96.2 12.5 %copy-start.15 = (bf16[1024,512]{1,0:T(8,128)(2,1)S(1)}, bf16[1024,512]{1,0:T(8,128)(2,1)}, u32[]{:S(2)}) copy-start(bf16[1024,512]{1,0:T(8,128)(2,1)} %param.11) | copy-start | bytes 3145732
  99.0 104.8 %collective-permute-start.3 = (bf16[3,768,512]{2,1,0:T(8,128)(2,1)}, bf16[3,768,512]{2,1,0:T(8,128)(2,1)}, u32[]{:S(2)}, u32[]{:S(2)}) collective-permute-start(bf16[3,768,512]{2,1,0:T(8,128)(2,1)} %get-tuple-element.344), channel_id=1, source_target_pairs={{0,8},{8,0},{16,24},{24,16},{1,9},{9,1},{17,25},{25,17},{2,10},{10... | collective-permute-start | bytes 7077896 | tf_op jit(solution)/shard_map/ppermute | solution.py:33
  100.5 299.6 %collective-permute-start.6 = (bf16[3,768,512]{2,1,0:T(8,128)(2,1)}, bf16[3,768,512]{2,1,0:T(8,128)(2,1)}, u32[]{:S(2)}, u32[]{:S(2)}) collective-permute-start(bf16[3,768,512]{2,1,0:T(8,128)(2,1)} %get-tuple-element.344), channel_id=1, source_target_pairs={{0,16},{8,24},{16,0},{24,8},{1,17},{9,25},{17,1},{25,9},{2,18},{10... | collective-permute-start | bytes 7077896 | tf_op jit(solution)/shard_map/ppermute | solution.py:33
  102.0 101.3 %collective-permute-start.4 = (bf16[3,768,512]{2,1,0:T(8,128)(2,1)}, bf16[3,768,512]{2,1,0:T(8,128)(2,1)}, u32[]{:S(2)}, u32[]{:S(2)}) collective-permute-start(bf16[3,768,512]{2,1,0:T(8,128)(2,1)} %get-tuple-element.345), channel_id=1, source_target_pairs={{0,16},{8,24},{16,0},{24,8},{1,17},{9,25},{17,1},{25,9},{2,18},{10... | collective-permute-start | bytes 7077896 | tf_op jit(solution)/shard_map/ppermute | solution.py:33
  102.5 308.1 %collective-permute-start.5 = (bf16[3,768,512]{2,1,0:T(8,128)(2,1)}, bf16[3,768,512]{2,1,0:T(8,128)(2,1)}, u32[]{:S(2)}, u32[]{:S(2)}) collective-permute-start(bf16[3,768,512]{2,1,0:T(8,128)(2,1)} %get-tuple-element.345), channel_id=1, source_target_pairs={{0,8},{8,0},{16,24},{24,16},{1,9},{9,1},{17,25},{25,17},{2,10},{10... | collective-permute-start | bytes 7077896 | tf_op jit(solution)/shard_map/ppermute | solution.py:33
  203.3 202.9 %collective-permute-start.7 = (bf16[3,768,512]{2,1,0:T(8,128)(2,1)}, bf16[3,768,512]{2,1,0:T(8,128)(2,1)S(1)}, u32[]{:S(2)}, u32[]{:S(2)}) collective-permute-start(bf16[3,768,512]{2,1,0:T(8,128)(2,1)} %collective-permute-done.4), channel_id=1, source_target_pairs={{0,8},{8,0},{16,24},{24,16},{1,9},{9,1},{17,25},{25,17},{2,10},{10... | collective-permute-start | bytes 7077896 | tf_op jit(solution)/shard_map/ppermute | solution.py:33
  203.8 213.0 %collective-permute-start.8 = (bf16[3,768,512]{2,1,0:T(8,128)(2,1)}, bf16[3,768,512]{2,1,0:T(8,128)(2,1)S(1)}, u32[]{:S(2)}, u32[]{:S(2)}) collective-permute-start(bf16[3,768,512]{2,1,0:T(8,128)(2,1)} %collective-permute-done.3), channel_id=1, source_target_pairs={{0,16},{8,24},{16,0},{24,8},{1,17},{9,25},{17,1},{25,9},{2,18},{10... | collective-permute-start | bytes 7077896 | tf_op jit(solution)/shard_map/ppermute | solution.py:33
  377.8 32.8 %copy-start = (bf16[128,8,8,768]{3,1,2,0:T(8,128)(2,1)}, bf16[128,8,8,768]{3,1,2,0:T(8,128)(2,1)S(1)}, u32[]{:S(2)}) copy-start(bf16[128,8,8,768]{3,1,2,0:T(8,128)(2,1)S(1)} %copy.193) | copy-start | bytes 37748740
  476.7 7.4 copy-start.20
  476.7 18.3 %collective-permute-start.10 = (bf16[9,128,128]{2,1,0:T(8,128)(2,1)}, bf16[9,128,128]{2,1,0:T(8,128)(2,1)S(1)}, u32[]{:S(2)}, u32[]{:S(2)}) collective-permute-start(bf16[9,128,128]{2,1,0:T(8,128)(2,1)} %pad_maximum_fusion.4), channel_id=1, source_target_pairs={{0,16},{8,24},{16,0},{24,8},{1,17},{9,25},{17,1},{25,9},{2,18},{10... | collective-permute-start | bytes 884744 | tf_op jit(solution)/shard_map/ppermute | solution.py:33
  478.1 16.9 %collective-permute-start.11 = (bf16[9,128,128]{2,1,0:T(8,128)(2,1)}, bf16[9,128,128]{2,1,0:T(8,128)(2,1)S(1)}, u32[]{:S(2)}, u32[]{:S(2)}) collective-permute-start(bf16[9,128,128]{2,1,0:T(8,128)(2,1)} %pad_maximum_fusion.4), channel_id=1, source_target_pairs={{0,8},{8,0},{16,24},{24,16},{1,9},{9,1},{17,25},{25,17},{2,10},{10... | collective-permute-start | bytes 884744 | tf_op jit(solution)/shard_map/ppermute | solution.py:33
  479.5 16.9 %collective-permute-start.9 = (bf16[9,128,128]{2,1,0:T(8,128)(2,1)}, bf16[9,128,128]{2,1,0:T(8,128)(2,1)}, u32[]{:S(2)}, u32[]{:S(2)}) collective-permute-start(bf16[9,128,128]{2,1,0:T(8,128)(2,1)} %pad_maximum_fusion.4), channel_id=1, source_target_pairs={{0,24},{8,16},{16,8},{24,0},{1,25},{9,17},{17,9},{25,1},{2,26},{10... | collective-permute-start | bytes 884744 | tf_op jit(solution)/shard_map/ppermute | solution.py:33
  520.3 11.5 %slice-start.7 = ((s8[4718592]{0:T(1024)(128)(4,1)}), s8[524288]{0:T(1024)(128)(4,1)S(1)}, s32[]{:S(2)}) async-start(s8[4718592]{0:T(1024)(128)(4,1)} %bitcast.288), calls=%async_computation.9 | async-start | bytes 1048576
  525.7 41.7 %copy-start.11 = (bf16[1,1024,512]{2,1,0:T(8,128)(2,1)}, bf16[1,1024,512]{2,1,0:T(8,128)(2,1)S(1)}, u32[]{:S(2)}) copy-start(bf16[1,1024,512]{2,1,0:T(8,128)(2,1)S(1)} %get-tuple-element.340) | copy-start | bytes 3145732
  525.7 6.1 slice-start.8
  573.1 12.9 %slice-start = ((s8[12582912]{0:T(1024)(128)(4,1)}), s8[4194304]{0:T(1024)(128)(4,1)S(1)}, s32[]{:S(2)}) async-start(s8[12582912]{0:T(1024)(128)(4,1)} %bitcast.272), calls=%async_computation.2 | async-start | bytes 8388608
  573.2 12.9 %slice-start.1 = ((s8[12582912]{0:T(1024)(128)(4,1)}), s8[4194304]{0:T(1024)(128)(4,1)S(1)}, s32[]{:S(2)}) async-start(s8[12582912]{0:T(1024)(128)(4,1)} %bitcast.272), calls=%async_computation.3 | async-start | bytes 8388608
  577.7 8.3 %slice-start.2 = ((s8[12582912]{0:T(1024)(128)(4,1)}), s8[4194304]{0:T(1024)(128)(4,1)S(1)}, s32[]{:S(2)}) async-start(s8[12582912]{0:T(1024)(128)(4,1)} %bitcast.272), calls=%async_computation.4 | async-start | bytes 8388608
  577.7 54.3 %collective-permute-start.13 = (bf16[3,768,512]{1,2,0:T(8,128)(2,1)S(1)}, bf16[3,768,512]{1,2,0:T(8,128)(2,1)S(1)}, u32[]{:S(2)}, u32[]{:S(2)}) collective-permute-start(bf16[3,768,512]{1,2,0:T(8,128)(2,1)S(1)} %convert_bitcast_fusion.2), channel_id=1, source_target_pairs={{0,8},{8,0},{16,24},{24,16},{1,9},{9,1},{17,25},{25,17},{2,10},{10... | collective-permute-start | bytes 7077896 | tf_op jit(solution)/shard_map/ppermute | solution.py:33
  584.2 54.3 %collective-permute-start.15 = (bf16[3,768,512]{1,2,0:T(8,128)(2,1)S(1)}, bf16[3,768,512]{1,2,0:T(8,128)(2,1)S(1)}, u32[]{:S(2)}, u32[]{:S(2)}) collective-permute-start(bf16[3,768,512]{1,2,0:T(8,128)(2,1)S(1)} %convert_bitcast_fusion.1), channel_id=1, source_target_pairs={{0,16},{8,24},{16,0},{24,8},{1,17},{9,25},{17,1},{25,9},{2,18},{10... | collective-permute-start | bytes 7077896 | tf_op jit(solution)/shard_map/ppermute | solution.py:33
  589.2 93.4 %collective-permute-start.12 = (bf16[3,768,512]{1,2,0:T(8,128)(2,1)S(1)}, bf16[3,768,512]{1,2,0:T(8,128)(2,1)S(1)}, u32[]{:S(2)}, u32[]{:S(2)}) collective-permute-start(bf16[3,768,512]{1,2,0:T(8,128)(2,1)S(1)} %convert_bitcast_fusion.3), channel_id=1, source_target_pairs={{0,8},{8,0},{16,24},{24,16},{1,9},{9,1},{17,25},{25,17},{2,10},{10... | collective-permute-start | bytes 7077896 | tf_op jit(solution)/shard_map/ppermute | solution.py:33
  593.5 143.6 %collective-permute-start.17 = (bf16[3,768,512]{1,2,0:T(8,128)(2,1)S(1)}, bf16[3,768,512]{1,2,0:T(8,128)(2,1)S(1)}, u32[]{:S(2)}, u32[]{:S(2)}) collective-permute-start(bf16[3,768,512]{1,2,0:T(8,128)(2,1)S(1)} %convert_bitcast_fusion), channel_id=1, source_target_pairs={{0,16},{8,24},{16,0},{24,8},{1,17},{9,25},{17,1},{25,9},{2,18},{10... | collective-permute-start | bytes 7077896 | tf_op jit(solution)/shard_map/ppermute | solution.py:33
  636.1 100.0 %collective-permute-start.14 = (bf16[3,768,512]{1,2,0:T(8,128)(2,1)}, bf16[3,768,512]{1,2,0:T(8,128)(2,1)S(1)}, u32[]{:S(2)}, u32[]{:S(2)}) collective-permute-start(bf16[3,768,512]{1,2,0:T(8,128)(2,1)} %fusion.9), channel_id=1, source_target_pairs={{0,16},{8,24},{16,0},{24,8},{1,17},{9,25},{17,1},{25,9},{2,18},{10... | collective-permute-start | bytes 7077896 | tf_op jit(solution)/shard_map/ppermute | solution.py:33
  642.8 94.2 %collective-permute-start.16 = (bf16[3,768,512]{1,2,0:T(8,128)(2,1)}, bf16[3,768,512]{1,2,0:T(8,128)(2,1)S(1)}, u32[]{:S(2)}, u32[]{:S(2)}) collective-permute-start(bf16[3,768,512]{1,2,0:T(8,128)(2,1)} %fusion.6), channel_id=1, source_target_pairs={{0,8},{8,0},{16,24},{24,16},{1,9},{9,1},{17,25},{25,17},{2,10},{10... | collective-permute-start | bytes 7077896 | tf_op jit(solution)/shard_map/ppermute | solution.py:33
  (21 other events, 60.2 us)
Sparse Core Ops, SparseCore 0:
  571.4 130.1 reduce-scatter.1
